TPU v7x, 32 devices: a whole 2x2x4 slice. The times are simulated.
32 devices in a mesh: groups: 2 (over x), segment: 4 (over y, core), head: 4 (over z).
Axes of the slice: x: 2, y: 2, z: 4, core: 2. Of those that a mesh axis runs over, the one named last changes fastest.
Arguments:
- token_ids: int32 [6, 256], P('groups'), parts along dimension 0, may hold values from 0 to 18991, as said below
- embed_table: bfloat16 [18992, 256], P(('segment', 'head')), may hold values from -6 to 6
- arriving: bfloat16 [8, 256, 256], P(('groups', 'segment')), parts along dimension 0, may hold values from -16 to 16
- returning: bfloat16 [8, 256, 256], P(('groups', 'segment')), parts along dimension 0, may hold values from -6 to 6
- stashed: bfloat16 [8, 3, 256, 256], P(('groups', 'segment')), parts along dimension 0, may hold values from -16 to 16
- seed_grad: bfloat16 [6, 256, 256], P('groups'), parts along dimension 0, may hold values from -6 to 6
- expand: bfloat16 [4, 256, 2048], P('segment'), may hold values from -0.375 to 0.375
- compress: bfloat16 [4, 2048, 256], P('segment'), may hold values from -0.125 to 0.125
- norm_gain: float32 [4, 2048], P('segment'), may hold values from 0.1 to 1.9
- w_query: bfloat16 [4, 2048, 4096], P('segment', None, 'head'), may hold values from -0.125 to 0.125
- key_weight: bfloat16 [4, 2048, 512], P('segment'), may hold values from -0.125 to 0.125
- value_weight: bfloat16 [4, 2048, 512], P('segment'), may hold values from -0.125 to 0.125
- w_out: bfloat16 [4, 4096, 2048], P('segment', 'head'), may hold values from -0.09375 to 0.09375
Outputs:
- sent_forward: bfloat16 [8, 3, 256, 256], P(('groups', 'segment'), None, 'head'), parts along dimension 0
- sent_backward: bfloat16 [8, 3, 256, 256], P(('groups', 'segment'), None, 'head'), parts along dimension 0
There are 2 independent parts, one for each index of `groups`. A program takes and returns all parts, laid end to end along the dimension named above; an argument that names none is the same for every part. Nothing has to cross between parts.
Inputs may be any that keep to these rules, and one draw needn't show every extreme that they name: `token_ids`: every aligned block of 1187 ids is named by some token.
All inputs are finite; a program needn't handle non-finite values.
Results may differ from a plain program's by a relative error of at most 0.02.
Values may be sent and summed in bfloat16 or wider, within the bound.
A program may use at most 128 MiB of HBM per device.

v0:
```python
import math
import jax
import jax.numpy as jnp
from jax import lax
from jax.sharding import PartitionSpec as P

QUERY_HEADS = 32
KEY_VALUE_HEADS = 4
HEAD_SIZE = 128
EPS = 1e-06


def passed_along(x, axis, by):
    length = lax.axis_size(axis)
    pairs = [(i, i + by) for i in range(length) if 0 <= i + by < length]
    return lax.ppermute(x, axis, pairs)


def rms_scale(matrix):
    return lax.rsqrt(jnp.mean(matrix * matrix, axis=-1, keepdims=True) + EPS)


def precise(former, latter):
    return jnp.dot(
        former, latter, precision=lax.Precision.HIGHEST, preferred_element_type=jnp.float32
    )


def precise_back(former, latter):
    return lax.dot_general(
        former,
        latter,
        (((1,), (1,)), ((), ())),
        precision=lax.Precision.HIGHEST,
        preferred_element_type=jnp.float32,
    )


def narrow_back(former, latter):
    return lax.dot_general(
        former, latter, (((1,), (1,)), ((), ())), preferred_element_type=jnp.float32
    )


def norm_back(upstream_in, grad_hat):
    scaling = rms_scale(upstream_in)
    return scaling * grad_hat - upstream_in * scaling**3 * jnp.mean(
        grad_hat * upstream_in, axis=-1, keepdims=True
    )


def section_inputs(coeffs, expand_here, gain_here, query_here, key_here, value_here):
    row_count = coeffs.shape[0]
    hidden = jnp.dot(coeffs, expand_here, preferred_element_type=jnp.float32)
    scaling = rms_scale(hidden)
    normed = (hidden * scaling * gain_here).astype(jnp.bfloat16)
    queries = jnp.dot(normed, query_here, preferred_element_type=jnp.float32).reshape(
        row_count, -1, HEAD_SIZE
    )
    key_rows = jnp.dot(normed, key_here, preferred_element_type=jnp.float32).reshape(
        row_count, -1, HEAD_SIZE
    )
    values = (
        jnp.dot(normed, value_here, preferred_element_type=jnp.float32)
        .astype(jnp.bfloat16)
        .reshape(row_count, -1, HEAD_SIZE)
    )
    q_hat = (queries * rms_scale(queries)).astype(jnp.bfloat16)
    k_hat = (key_rows * rms_scale(key_rows)).astype(jnp.bfloat16)
    return (hidden, scaling, queries, key_rows, q_hat, k_hat, values)


def probabilities(q_hat, k_hat):
    row_count, head_count, head_width = q_hat.shape
    kv_heads = k_hat.shape[1]
    grouped = q_hat.reshape(row_count, kv_heads, head_count // kv_heads, head_width)
    scores = jnp.einsum(
        "iknd,jkd->knij", grouped, k_hat, preferred_element_type=jnp.float32
    ) / math.sqrt(head_width)
    causal = jnp.arange(row_count)[None, :] <= jnp.arange(row_count)[:, None]
    weights = jnp.where(causal, jnp.exp(scores), 0.0)
    return weights / jnp.sum(weights, axis=-1, keepdims=True)


def section_forward(coeffs, expand_here, gain_here, query_here, key_here, value_here, out_folded):
    hidden, scaling, queries, key_rows, q_hat, k_hat, values = section_inputs(
        coeffs, expand_here, gain_here, query_here, key_here, value_here
    )
    weights = probabilities(q_hat, k_hat)
    attended = jnp.einsum(
        "knij,jkd->iknd", weights.astype(jnp.bfloat16), values, preferred_element_type=jnp.float32
    )
    attended = attended.reshape(coeffs.shape[0], -1).astype(jnp.bfloat16)
    return jnp.dot(attended, out_folded, preferred_element_type=jnp.float32)


def section_backward(
    coeffs, grads, expand_here, gain_here, query_here, key_here, value_here, out_folded
):
    row_count = coeffs.shape[0]
    hidden, scaling, queries, key_rows, q_hat, k_hat, values = section_inputs(
        coeffs, expand_here, gain_here, query_here, key_here, value_here
    )
    weights = probabilities(q_hat, k_hat)
    head_count = queries.shape[1]
    kv_heads = key_rows.shape[1]
    query_group_size = head_count // kv_heads
    grad_attended = narrow_back(grads, out_folded).astype(jnp.bfloat16)
    grad_attended = grad_attended.reshape(row_count, kv_heads, query_group_size, HEAD_SIZE)
    grad_weights = jnp.einsum(
        "iknd,jkd->knij", grad_attended, values, preferred_element_type=jnp.float32
    )
    grad_scores = (
        weights
        * (grad_weights - jnp.sum(grad_weights * weights, axis=-1, keepdims=True))
        / math.sqrt(HEAD_SIZE)
    )
    grad_scores = grad_scores.astype(jnp.bfloat16)
    grouped = q_hat.reshape(row_count, kv_heads, query_group_size, HEAD_SIZE)
    grad_qhat = jnp.einsum(
        "knij,jkd->iknd", grad_scores, k_hat, preferred_element_type=jnp.float32
    ).reshape(row_count, head_count, HEAD_SIZE)
    grad_khat = jnp.einsum(
        "knij,iknd->jkd", grad_scores, grouped, preferred_element_type=jnp.float32
    )
    grad_values = jnp.einsum(
        "knij,iknd->jkd",
        weights.astype(jnp.bfloat16),
        grad_attended,
        preferred_element_type=jnp.float32,
    )
    grad_values = grad_values.reshape(row_count, -1).astype(jnp.bfloat16)
    grad_queries = norm_back(queries, grad_qhat).reshape(row_count, -1).astype(jnp.bfloat16)
    grad_keys = norm_back(key_rows, grad_khat).reshape(row_count, -1).astype(jnp.bfloat16)
    grad_normed = (
        narrow_back(grad_queries, query_here)
        + narrow_back(grad_keys, key_here)
        + narrow_back(grad_values, value_here)
    )
    weighted = grad_normed * gain_here
    grad_hidden = scaling * weighted - hidden * scaling**3 * jnp.mean(
        weighted * hidden, axis=-1, keepdims=True
    )
    return narrow_back(grad_hidden.astype(jnp.bfloat16), expand_here)


def shards(
    token_ids,
    embed_table,
    arriving,
    returning,
    stashed,
    seed_grad,
    expand,
    compress,
    norm_gain,
    w_query,
    key_weight,
    value_weight,
    w_out,
):
    segment_index = lax.axis_index("segment")
    last_segment = lax.axis_size("segment") - 1
    head_index = lax.axis_index("head")
    heads_here = w_query.shape[2] // HEAD_SIZE
    query_group_size = QUERY_HEADS // KEY_VALUE_HEADS
    kv_here = (heads_here + query_group_size - 1) // query_group_size
    first_kv = head_index * heads_here // query_group_size
    expand_here = expand[0]
    gain_here = norm_gain[0]
    query_here = w_query[0]
    key_here = lax.dynamic_slice_in_dim(key_weight[0], first_kv * HEAD_SIZE, kv_here * HEAD_SIZE, 1)
    value_here = lax.dynamic_slice_in_dim(
        value_weight[0], first_kv * HEAD_SIZE, kv_here * HEAD_SIZE, 1
    )
    basis_folded = jnp.dot(expand_here, compress[0], preferred_element_type=jnp.float32)
    out_folded = jnp.dot(w_out[0], compress[0], preferred_element_type=jnp.float32).astype(
        jnp.bfloat16
    )
    table_rows = embed_table.shape[0]
    local_ids = token_ids.reshape(-1) - lax.axis_index(("segment", "head")) * table_rows
    inside = (local_ids >= 0) & (local_ids < table_rows)
    looked = jnp.take(embed_table, jnp.clip(local_ids, 0, table_rows - 1), axis=0).astype(
        jnp.float32
    )
    picked = jnp.where(inside[:, None], looked, 0.0)
    embedded = lax.psum(picked, ("segment", "head")).astype(jnp.bfloat16)
    tick_count = token_ids.shape[0]
    span_rows = token_ids.shape[1]
    embedded = embedded.reshape(tick_count, span_rows, -1)
    share_rows = span_rows // lax.axis_size("head")
    share_start = head_index * share_rows
    forward_recv = arriving[0]
    backward_recv = returning[0]
    history = []
    forward_shares = []
    backward_shares = []
    for tick_index in range(tick_count):
        more_ticks = tick_index + 1 < tick_count
        forward_in = jnp.where(segment_index == 0, embedded[tick_index], forward_recv)
        backward_in = jnp.where(segment_index == last_segment, seed_grad[tick_index], backward_recv)
        history.append(forward_in)
        delay_ticks = 2 * (last_segment - segment_index)
        replay = stashed[0, tick_index]
        for earlier in range(tick_index + 1):
            replay = jnp.where(delay_ticks == tick_index - earlier, history[earlier], replay)
        partial_value = section_forward(
            forward_in, expand_here, gain_here, query_here, key_here, value_here, out_folded
        )
        direct = precise(forward_in.astype(jnp.float32), basis_folded)
        summed = lax.psum_scatter(
            partial_value.astype(jnp.bfloat16), "head", scatter_dimension=0, tiled=True
        ).astype(jnp.float32)
        own_rows = (summed + lax.dynamic_slice_in_dim(direct, share_start, share_rows, 0)).astype(
            jnp.bfloat16
        )
        forward_shares.append(own_rows)
        if more_ticks:
            arrived = passed_along(own_rows, "segment", 1)
            forward_recv = lax.all_gather(arrived, "head", axis=0, tiled=True)
        partial_back = section_backward(
            replay,
            backward_in,
            expand_here,
            gain_here,
            query_here,
            key_here,
            value_here,
            out_folded,
        )
        direct_back = precise_back(backward_in.astype(jnp.float32), basis_folded)
        summed_back = lax.psum_scatter(
            partial_back.astype(jnp.bfloat16), "head", scatter_dimension=0, tiled=True
        ).astype(jnp.float32)
        own_back = (
            summed_back + lax.dynamic_slice_in_dim(direct_back, share_start, share_rows, 0)
        ).astype(jnp.bfloat16)
        backward_shares.append(own_back)
        if more_ticks:
            arrived_back = passed_along(own_back, "segment", -1)
            backward_recv = lax.all_gather(arrived_back, "head", axis=0, tiled=True)
    sent_forward = jnp.stack(forward_shares)[None]
    sent_backward = jnp.stack(backward_shares)[None]
    return (sent_forward, sent_backward)


def solution(mesh):
    return jax.shard_map(
        shards,
        mesh=mesh,
        in_specs=(
            P("groups", None),
            P(("segment", "head"), None),
            P(("groups", "segment"), None, None),
            P(("groups", "segment"), None, None),
            P(("groups", "segment"), None, None, None),
            P("groups", None, None),
            P("segment", None, None),
            P("segment", None, None),
            P("segment", None),
            P("segment", None, "head"),
            P("segment", None, None),
            P("segment", None, None),
            P("segment", "head", None),
        ),
        out_specs=(
            P(("groups", "segment"), None, "head", None),
            P(("groups", "segment"), None, "head", None),
        ),
        check_vma=False,
    )
```

profile of v0, /device:TPU:0, one launch (start us, length us, event | category | flops | bytes accessed | tf_op | source)
XLA Modules:
  0.0 454.7 jit_solution(9600917615611538147)
XLA Ops:
  9.6 4.0 gather_fusion
  15.9 78.0 %all-reduce.1 = bf16[768,256]{1,0:T(8,128)(2,1)} all-reduce(f32[768,256]{1,0:T(8,128)} %convert_select_fusion), channel_id=1, replica_groups=mesh['groups'=2,'segment'=4,'head'=4] {'segment','head'}, use_global_device_ids=true, to_apply=%region_0.1 | all-reduce | flops 196608 | bytes 1179648 | tf_op jit(solution)/shard_map/psum | solution.py:187
  101.1 6.5 %copy.87 = bf16[1024,2048]{1,0:T(8,128)(2,1)} copy(bf16[1024,2048]{0,1:T(8,128)(2,1)} %bitcast.659) | data formatting | bytes 8388608 | tf_op jit(solution)/shard_map/dot_general | solution.py:57
  107.6 4.0 multiply_reduce_fusion.17
  131.3 9.0 %reduce-scatter.7.cloned.1.call-done = bf16[64,256]{1,0:T(8,128)(2,1)} async-done(((bf16[256,256]{1,0:T(8,128)(2,1)}), bf16[64,256]{1,0:T(8,128)(2,1)}) %reduce-scatter.7.cloned.1.call-update) | async-done | bytes 32784 | tf_op jit(solution)/shard_map/reduce_scatter | solution.py:211
  146.1 13.8 %all_gather.12 = bf16[256,256]{1,0:T(8,128)(2,1)S(1)} all-gather(bf16[64,256]{1,0:T(8,128)(2,1)} %collective-permute-done), channel_id=1, replica_groups=mesh['groups'=2,'segment'=4,'head'=4] {'head'}, dimensions={0}, use_global_device_ids=true | all-gather | bytes 163840 | tf_op jit(solution)/shard_map/all_gather | solution.py:220
  179.6 3.8 convolution_convert_fusion.4
  192.2 12.4 %reduce-scatter.9.cloned.1.call-done = bf16[64,256]{1,0:T(8,128)(2,1)} async-done(((bf16[256,256]{1,0:T(8,128)(2,1)}), bf16[64,256]{1,0:T(8,128)(2,1)}) %reduce-scatter.9.cloned.1.call-update) | async-done | bytes 32784 | tf_op jit(solution)/shard_map/reduce_scatter | solution.py:211
  208.6 13.7 %all_gather.13 = bf16[256,256]{1,0:T(8,128)(2,1)S(1)} all-gather(bf16[64,256]{1,0:T(8,128)(2,1)S(1)} %collective-permute-done.1), channel_id=1, replica_groups=mesh['groups'=2,'segment'=4,'head'=4] {'head'}, dimensions={0}, use_global_device_ids=true | all-gather | bytes 163840 | tf_op jit(solution)/shard_map/all_gather | solution.py:220
  235.5 5.0 %fusion.19 = (f32[8,256]{1,0:T(8,128)}, f32[256,256,8]{1,0,2:T(8,128)}) fusion(f32[8,256]{1,0:T(8,128)S(1)} %get-tuple-element.5, f32[256,256,8]{1,0,2:T(8,128)} %fusion.141, pred[256,256]{0,1:T(8,128)(4,1)S(1)} %copy-done.28, bf16[256,2048]{1,0:T(8,128)(2,1)} %copy-done.13, bf16[1,2048,512]{2,1,0:T(8,128)(2,1)S(1)} %copy-done, s32[]{:T(128)S(6)} %select_n.142, ...), kind=kOutput, calls=%fused_computation.38 | convolution fusion | flops 271087616 | bytes 6373380 | tf_op jit(solution)/shard_map/iknd,jkd->knij/dot_general | solution.py:110
  240.4 4.1 convert_bitcast_fusion.2
  263.7 5.1 %multiply_reduce_fusion.4 = (f32[256]{0:T(256)S(1)}, f32[256,2048]{1,0:T(8,128)}) fusion(f32[256,2048]{1,0:T(8,128)} %get-tuple-element.49, f32[2048]{0:T(1024)S(1)} %bitcast.678, f32[256,2048]{1,0:T(8,128)} %convolution_add_fusion.5, bf16[1,2048,512]{2,1,0:T(8,128)(2,1)S(1)} %copy-done, s32[]{:T(128)S(6)} %select_n.142, ...), kind=kOutput, calls=%fused_computation.51 | convolution fusion | flops 270565120 | bytes 8397828 | tf_op jit(solution)/shard_map/dot_general | solution.py:40
  276.1 16.2 %reduce-scatter.13.cloned.1.call-done = bf16[64,256]{1,0:T(8,128)(2,1)} async-done(((bf16[256,256]{1,0:T(8,128)(2,1)}), bf16[64,256]{1,0:T(8,128)(2,1)}) %reduce-scatter.13.cloned.1.call-update) | async-done | bytes 32784 | tf_op jit(solution)/shard_map/reduce_scatter | solution.py:232
  296.2 13.5 %all_gather.14 = bf16[256,256]{1,0:T(8,128)(2,1)S(1)} all-gather(bf16[64,256]{1,0:T(8,128)(2,1)S(1)} %collective-permute-done.2), channel_id=1, replica_groups=mesh['groups'=2,'segment'=4,'head'=4] {'head'}, dimensions={0}, use_global_device_ids=true | all-gather | bytes 163840 | tf_op jit(solution)/shard_map/all_gather | solution.py:241
  312.6 5.0 %fusion.15 = (f32[8,256]{1,0:T(8,128)}, f32[256,256,8]{1,0,2:T(8,128)}) fusion(f32[8,256]{1,0:T(8,128)} %get-tuple-element.6, f32[256,256,8]{1,0,2:T(8,128)} %copy-done.10, pred[256,256]{0,1:T(8,128)(4,1)S(1)} %copy-done.29, bf16[256,2048]{1,0:T(8,128)(2,1)} %copy-done.12, bf16[1,2048,512]{2,1,0:T(8,128)(2,1)S(1)} %copy-done, s32[]{:T(128)S(6)} %select_n.142, ...), kind=kOutput, calls=%fused_computation.32 | convolution fusion | flops 271087616 | bytes 6373380 | tf_op jit(solution)/shard_map/iknd,jkd->knij/dot_general | solution.py:110
  317.6 4.0 convert_bitcast_fusion.1
  338.3 5.1 %multiply_reduce_fusion.2 = (f32[256]{0:T(256)S(1)}, f32[256,2048]{1,0:T(8,128)}) fusion(f32[256,2048]{1,0:T(8,128)} %copy-done.3, f32[2048]{0:T(1024)S(1)} %bitcast.679, f32[256,2048]{1,0:T(8,128)} %convolution_add_fusion.3, bf16[1,2048,512]{2,1,0:T(8,128)(2,1)S(1)} %copy-done, s32[]{:T(128)S(6)} %select_n.142, bf16[256,8,128]{2,1,0:T(8,128)(2,1)} %bitcast.671, ...), kind=kOutput, calls=%fused_computation.47 | convolution fusion | flops 270565120 | bytes 8397828 | tf_op jit(solution)/shard_map/dot_general | solution.py:40
  352.1 12.9 %reduce-scatter.15.cloned.1.call-done = bf16[64,256]{1,0:T(8,128)(2,1)} async-done(((bf16[256,256]{1,0:T(8,128)(2,1)}), bf16[64,256]{1,0:T(8,128)(2,1)}) %reduce-scatter.15.cloned.1.call-update) | async-done | bytes 32784 | tf_op jit(solution)/shard_map/reduce_scatter | solution.py:232
  369.3 13.6 %all_gather.15 = bf16[256,256]{1,0:T(8,128)(2,1)S(1)} all-gather(bf16[64,256]{1,0:T(8,128)(2,1)S(1)} %collective-permute-done.3), channel_id=1, replica_groups=mesh['groups'=2,'segment'=4,'head'=4] {'head'}, dimensions={0}, use_global_device_ids=true | all-gather | bytes 163840 | tf_op jit(solution)/shard_map/all_gather | solution.py:241
  385.8 5.4 %fusion.11 = (f32[8,256]{1,0:T(8,128)S(1)}, f32[8,256]{1,0:T(8,128)S(1)}, f32[256,256,8]{1,0,2:T(8,128)}) fusion(f32[8,256]{1,0:T(8,128)S(1)} %copy-done.68, f32[256,256,8]{1,0,2:T(8,128)} %get-tuple-element.76, pred[256,256]{0,1:T(8,128)(4,1)S(1)} %copy-done.30, f32[256,256,8]{1,0,2:T(8,128)} %fusion.101, bf16[256,2048]{1,0:T(8,128)(2,1)} %copy-done.20, ...), kind=kOutput, calls=%fused_computation.26 | convolution fusion | flops 272658432 | bytes 8478724 | tf_op jit(solution)/shard_map/iknd,jkd->knij/dot_general | solution.py:110
  391.2 4.0 convert_bitcast_fusion
  398.6 3.8 convolution_convert_fusion.3
  415.6 5.1 %multiply_reduce_fusion = (f32[256]{0:T(256)S(1)}, f32[256,2048]{1,0:T(8,128)}) fusion(f32[256,2048]{1,0:T(8,128)} %copy-done.2, f32[2048]{0:T(1024)S(1)} %bitcast.680, f32[256,2048]{1,0:T(8,128)} %convolution_add_fusion.1, bf16[1,2048,512]{2,1,0:T(8,128)(2,1)S(1)} %copy-done, s32[]{:T(128)S(6)} %select_n.142, bf16[256,8,128]{2,1,0:T(8,128)(2,1)} %bitcast.670, ...), kind=kOutput, calls=%fused_computation.43 | convolution fusion | flops 270565120 | bytes 8397828 | tf_op jit(solution)/shard_map/dot_general | solution.py:40
  428.0 17.6 %reduce-scatter.17.cloned.1.call-done = bf16[64,256]{1,0:T(8,128)(2,1)} async-done(((bf16[256,256]{1,0:T(8,128)(2,1)}), bf16[64,256]{1,0:T(8,128)(2,1)}) %reduce-scatter.17.cloned.1.call-update) | async-done | bytes 32784 | tf_op jit(solution)/shard_map/reduce_scatter | solution.py:232
  (290 shorter events, 174.1 us)
Async XLA Ops:
  7.2 108.5 %copy-start = (bf16[1,2048,512]{2,1,0:T(8,128)(2,1)S(1)}, bf16[1,2048,512]{2,1,0:T(8,128)(2,1)}, u32[]{:S(2)}) copy-start(bf16[1,2048,512]{2,1,0:T(8,128)(2,1)} %param.24) | copy-start | bytes 6291460
  7.2 133.1 %reduce-scatter.7.cloned.1.call-start = ((), (), s32[]{:S(2)}) async-start(), calls=%async_computation.6 | async-start | bytes 163840 | tf_op jit(solution)/shard_map/reduce_scatter | solution.py:211
  9.5 106.2 %copy-start.26 = (pred[256,256]{0,1:T(8,128)(4,1)}, pred[256,256]{0,1:T(8,128)(4,1)S(1)}, u32[]{:S(2)}) copy-start(pred[256,256]{0,1:T(8,128)(4,1)S(1)} %iota_compare_fusion) | copy-start | bytes 196612
  9.6 84.3 %copy-start.49 = (bf16[1,256,256]{2,1,0:T(8,128)(2,1)S(1)}, bf16[1,256,256]{2,1,0:T(8,128)(2,1)}, u32[]{:S(2)}) copy-start(bf16[1,256,256]{2,1,0:T(8,128)(2,1)} %param.15) | copy-start | bytes 393220
  13.6 81.3 %copy-start.1 = (bf16[1,256,2048]{2,1,0:T(8,128)(2,1)S(1)}, bf16[1,256,2048]{2,1,0:T(8,128)(2,1)}, u32[]{:S(2)}) copy-start(bf16[1,256,2048]{2,1,0:T(8,128)(2,1)} %param.19) | copy-start | bytes 3145732
  121.6 83.0 %reduce-scatter.9.cloned.1.call-start = ((), (), s32[]{:S(2)}) async-start(), calls=%async_computation.7 | async-start | bytes 163840 | tf_op jit(solution)/shard_map/reduce_scatter | solution.py:211
  141.8 4.4 collective-permute-start
  144.2 19.5 %copy-start.66 = (f32[256]{0:T(256)}, f32[256]{0:T(256)S(1)}, u32[]{:S(2)}) copy-start(f32[256]{0:T(256)S(1)} %get-tuple-element.33) | copy-start | bytes 3076
  164.4 6.2 %copy-start.14 = (bf16[256,2048]{1,0:T(8,128)(2,1)}, bf16[256,2048]{1,0:T(8,128)(2,1)S(1)}, u32[]{:S(2)}) copy-start(bf16[256,2048]{1,0:T(8,128)(2,1)S(1)} %get-tuple-element.20) | copy-start | bytes 3145732
  164.4 8.6 %copy-start.13 = (bf16[256,2048]{1,0:T(8,128)(2,1)}, bf16[256,2048]{1,0:T(8,128)(2,1)S(1)}, u32[]{:S(2)}) copy-start(bf16[256,2048]{1,0:T(8,128)(2,1)S(1)} %get-tuple-element.21) | copy-start | bytes 3145732
  185.6 106.6 %reduce-scatter.13.cloned.1.call-start = ((), (), s32[]{:S(2)}) async-start(), calls=%async_computation.9 | async-start | bytes 163840 | tf_op jit(solution)/shard_map/reduce_scatter | solution.py:232
  205.5 3.1 collective-permute-start.1
  208.5 23.6 %copy-start.10 = (f32[256,256,8]{1,0,2:T(8,128)}, f32[256,256,8]{1,0,2:T(8,128)S(1)}, u32[]{:S(2)}) copy-start(f32[256,256,8]{1,0,2:T(8,128)S(1)} %fusion.142) | copy-start | bytes 6291460
  208.6 15.2 %copy-start.23 = (bf16[256,256]{1,0:T(8,128)(2,1)S(1)}, bf16[256,256]{1,0:T(8,128)(2,1)}, u32[]{:S(2)}) copy-start(bf16[256,256]{1,0:T(8,128)(2,1)} %copy-done.21) | copy-start | bytes 393220
  272.3 40.3 %copy-start.29 = (pred[256,256]{0,1:T(8,128)(4,1)S(1)}, pred[256,256]{0,1:T(8,128)(4,1)}, u32[]{:S(2)}) copy-start(pred[256,256]{0,1:T(8,128)(4,1)} %copy-done.26) | copy-start | bytes 196612
  272.3 92.7 %reduce-scatter.15.cloned.1.call-start = ((), (), s32[]{:S(2)}) async-start(), calls=%async_computation.10 | async-start | bytes 163840 | tf_op jit(solution)/shard_map/reduce_scatter | solution.py:232
  293.1 24.5 %copy-start.51 = (bf16[64,256]{1,0:T(8,128)(2,1)}, bf16[64,256]{1,0:T(8,128)(2,1)S(1)}, u32[]{:S(2)}) copy-start(bf16[64,256]{1,0:T(8,128)(2,1)S(1)} %add_convert_fusion.2) | copy-start | bytes 98308
  293.1 3.1 collective-permute-start.2
  347.0 78.7 %reduce-scatter.11.cloned.1.call-start = ((), (), s32[]{:S(2)}) async-start(), calls=%async_computation.8 | async-start | bytes 163840 | tf_op jit(solution)/shard_map/reduce_scatter | solution.py:211
  350.1 35.7 %copy-start.30 = (pred[256,256]{0,1:T(8,128)(4,1)S(1)}, pred[256,256]{0,1:T(8,128)(4,1)}, u32[]{:S(2)}) copy-start(pred[256,256]{0,1:T(8,128)(4,1)} %copy-done.26) | copy-start | bytes 196612
  350.1 35.7 %copy-start.68 = (f32[8,256]{1,0:T(8,128)S(1)}, f32[8,256]{1,0:T(8,128)}, u32[]{:S(2)}) copy-start(f32[8,256]{1,0:T(8,128)} %get-tuple-element.4) | copy-start | bytes 24580
  365.9 25.3 %copy-start.52 = (bf16[64,256]{1,0:T(8,128)(2,1)}, bf16[64,256]{1,0:T(8,128)(2,1)S(1)}, u32[]{:S(2)}) copy-start(bf16[64,256]{1,0:T(8,128)(2,1)S(1)} %add_convert_fusion.1) | copy-start | bytes 98308
  365.9 3.4 collective-permute-start.3
  407.2 38.3 %reduce-scatter.17.cloned.1.call-start = ((), (), s32[]{:S(2)}) async-start(), calls=%async_computation.11 | async-start | bytes 163840 | tf_op jit(solution)/shard_map/reduce_scatter | solution.py:232
  (64 other events, 207.1 us)
Sparse Core Ops, SparseCore 0:
  121.7 18.5 reduce-scatter.6
  185.7 18.8 reduce-scatter.8
  272.5 19.7 reduce-scatter.12
  347.1 17.8 reduce-scatter.14
  407.3 18.2 reduce-scatter.10
  427.8 17.6 reduce-scatter.16
where the time goes:
time: 463 us; the launch traced here: 455 us
  matrix products  156 us (34%)
  blocking collectives  133 us (29%)
  waiting for transfers between devices  69 us (15%)
  other arithmetic  47.6 us (10%)
  local copies, waits for them, and re-layouts  27.8 us (6%)
  between operations  15.2 us (3%)
  starting transfers between devices  6.18 us (1%)
    psum x1, blocking collectives, shards(): embedded = lax.psum(picked, ('segment', 'head')).astype(jnp.bfloat16)  78 us
    dot_general x15, matrix products, narrow_back(): lax.dot_general(former, latter, (((1,), (1,)), ((), ())), preferred_eleme...  51.8 us
    reduce_scatter x3, waiting for transfers between devices, shards(): lax.psum_scatter(partial_back.astype(jnp.bfloat16), 'head', scatter_dimen...  46.7 us
    all_gather x2, blocking collectives, shards(): forward_recv = lax.all_gather(arrived, 'head', axis=0, tiled=True)  27.6 us
    all_gather x2, blocking collectives, shards(): backward_recv = lax.all_gather(arrived_back, 'head', axis=0, tiled=True)  27.1 us
    reduce_scatter x3, waiting for transfers between devices, shards(): lax.psum_scatter(partial_value.astype(jnp.bfloat16), 'head', scatter_dime...  21.6 us
    dot_general x6, matrix products, probabilities(): jnp.einsum('iknd,jkd->knij', grouped, k_hat, preferred_element_type=jnp.f...  15.6 us
    dot_general x3, matrix products, section_backward(): jnp.einsum('iknd,jkd->knij', grad_attended, values, preferred_element_typ...  15.3 us
  transfers between devices with their start and end apart: 10, of which 7 were waited for; matrix products, arithmetic and copies ran while one was open for 11% of the time, Pallas kernels for 0%

commit v1 on v0

--- a/solution.py
+++ b/solution.py
@@ -184,7 +184,7 @@
         jnp.float32
     )
     picked = jnp.where(inside[:, None], looked, 0.0)
-    embedded = lax.psum(picked, ("segment", "head")).astype(jnp.bfloat16)
+    embedded = lax.psum(lax.psum(picked, "head"), "segment").astype(jnp.bfloat16)
     tick_count = token_ids.shape[0]
     span_rows = token_ids.shape[1]
     embedded = embedded.reshape(tick_count, span_rows, -1)

time: 463 us -> 435 us (0.940)
  blocking collectives: 133 us -> 74.7 us
  waiting for transfers between devices: 69 us -> 107 us
    psum x1, blocking collectives: 78 us -> 20.3 us  [shards(): lax.psum(lax.psum(picked, 'head'), 'segment').astype(jnp.bfloat16)]
    psum x0 -> x1, waiting for transfers between devices: none -> 29.6 us  [shards(): lax.psum(picked, 'head')]
    reduce_scatter x3, waiting for transfers between devices: 21.6 us -> 29.4 us  [shards(): lax.psum_scatter(partial_value.astype(jnp.bfloat16), 'head', scatter_dime...]
  transfers between devices with their start and end apart: 10 -> 11, of which waited for: 7 -> 9; matrix products, arithmetic and copies ran while one was open for 11% -> 14% of each run, Pallas kernels for 0% -> 0%
where the time goes in v1:
time: 435 us; the launch traced here: 427 us
  matrix products  154 us (35%)
  waiting for transfers between devices  107 us (25%)
  blocking collectives  74.7 us (17%)
  other arithmetic  45.2 us (10%)
  local copies, waits for them, and re-layouts  25.4 us (6%)
  between operations  15.2 us (3%)
  starting transfers between devices  5.63 us (1%)
    dot_general x15, matrix products, narrow_back(): lax.dot_general(former, latter, (((1,), (1,)), ((), ())), preferred_eleme...  50.9 us
    reduce_scatter x3, waiting for transfers between devices, shards(): lax.psum_scatter(partial_back.astype(jnp.bfloat16), 'head', scatter_dimen...  46.8 us
    psum x1, waiting for transfers between devices, shards(): lax.psum(picked, 'head')  29.6 us
    reduce_scatter x3, waiting for transfers between devices, shards(): lax.psum_scatter(partial_value.astype(jnp.bfloat16), 'head', scatter_dime...  29.4 us
    all_gather x2, blocking collectives, shards(): forward_recv = lax.all_gather(arrived, 'head', axis=0, tiled=True)  27.3 us
    all_gather x2, blocking collectives, shards(): backward_recv = lax.all_gather(arrived_back, 'head', axis=0, tiled=True)  27.1 us
    psum x1, blocking collectives, shards(): lax.psum(lax.psum(picked, 'head'), 'segment').astype(jnp.bfloat16)  20.3 us
    dot_general x6, matrix products, probabilities(): jnp.einsum('iknd,jkd->knij', grouped, k_hat, preferred_element_type=jnp.f...  15.6 us
  transfers between devices with their start and end apart: 11, of which 9 were waited for; matrix products, arithmetic and copies ran while one was open for 14% of the time, Pallas kernels for 0%

profile of v1, /device:TPU:0, one launch (start us, length us, event | category | flops | bytes accessed | tf_op | source)
XLA Modules:
  0.0 426.6 jit_solution(5563716105099990430)
XLA Ops:
  14.1 3.8 fusion.32
  20.3 6.7 %copy.87 = bf16[1024,2048]{1,0:T(8,128)(2,1)} copy(bf16[1024,2048]{0,1:T(8,128)(2,1)} %bitcast.659) | data formatting | bytes 8388608 | tf_op jit(solution)/shard_map/dot_general | solution.py:57
  31.2 29.6 %all-reduce.3.cloned.1.call-done = f32[768,256]{1,0:T(8,128)} async-done(((f32[768,256]{1,0:T(8,128)}), f32[768,256]{1,0:T(8,128)}) %all-reduce.3.cloned.1.call-update) | async-done | bytes 786448 | tf_op jit(solution)/shard_map/psum | solution.py:187
  60.8 20.3 %all-reduce.4 = bf16[768,256]{1,0:T(8,128)(2,1)} all-reduce(f32[768,256]{1,0:T(8,128)} %all-reduce.3.cloned.1.call-done), channel_id=1, replica_groups=mesh['groups'=2,'segment'=4,'head'=4] {'segment'}, use_global_device_ids=true, to_apply=%region_1.2 | all-reduce | flops 196608 | bytes 1179648 | tf_op jit(solution)/shard_map/psum | solution.py:187
  98.3 14.7 %reduce-scatter.7.cloned.1.call-done = bf16[64,256]{1,0:T(8,128)(2,1)} async-done(((bf16[256,256]{1,0:T(8,128)(2,1)}), bf16[64,256]{1,0:T(8,128)(2,1)}) %reduce-scatter.7.cloned.1.call-update) | async-done | bytes 32784 | tf_op jit(solution)/shard_map/reduce_scatter | solution.py:211
  116.0 13.6 %all_gather.12 = bf16[256,256]{1,0:T(8,128)(2,1)S(1)} all-gather(bf16[64,256]{1,0:T(8,128)(2,1)S(1)} %collective-permute-done), channel_id=1, replica_groups=mesh['groups'=2,'segment'=4,'head'=4] {'head'}, dimensions={0}, use_global_device_ids=true | all-gather | bytes 163840 | tf_op jit(solution)/shard_map/all_gather | solution.py:220
  149.3 3.8 convolution_convert_fusion.4
  162.0 14.4 %reduce-scatter.9.cloned.1.call-done = bf16[64,256]{1,0:T(8,128)(2,1)} async-done(((bf16[256,256]{1,0:T(8,128)(2,1)}), bf16[64,256]{1,0:T(8,128)(2,1)}) %reduce-scatter.9.cloned.1.call-update) | async-done | bytes 32784 | tf_op jit(solution)/shard_map/reduce_scatter | solution.py:211
  180.3 13.7 %all_gather.13 = bf16[256,256]{1,0:T(8,128)(2,1)S(1)} all-gather(bf16[64,256]{1,0:T(8,128)(2,1)S(1)} %collective-permute-done.1), channel_id=1, replica_groups=mesh['groups'=2,'segment'=4,'head'=4] {'head'}, dimensions={0}, use_global_device_ids=true | all-gather | bytes 163840 | tf_op jit(solution)/shard_map/all_gather | solution.py:220
  207.1 5.0 %fusion.19 = (f32[8,256]{1,0:T(8,128)}, f32[256,256,8]{1,0,2:T(8,128)}) fusion(f32[8,256]{1,0:T(8,128)S(1)} %get-tuple-element.5, f32[256,256,8]{1,0,2:T(8,128)} %fusion.141, pred[256,256]{0,1:T(8,128)(4,1)S(1)} %copy-done.30, bf16[256,2048]{1,0:T(8,128)(2,1)} %copy-done.14, bf16[1,2048,512]{2,1,0:T(8,128)(2,1)S(1)} %copy-done, s32[]{:T(128)S(6)} %select_n.142, ...), kind=kOutput, calls=%fused_computation.38 | convolution fusion | flops 271087616 | bytes 6373380 | tf_op jit(solution)/shard_map/iknd,jkd->knij/dot_general | solution.py:110
  212.1 4.1 convert_bitcast_fusion.2
  235.4 5.1 %multiply_reduce_fusion.4 = (f32[256]{0:T(256)S(1)}, f32[256,2048]{1,0:T(8,128)}) fusion(f32[256,2048]{1,0:T(8,128)} %get-tuple-element.49, f32[2048]{0:T(1024)S(1)} %bitcast.678, f32[256,2048]{1,0:T(8,128)} %convolution_add_fusion.5, bf16[1,2048,512]{2,1,0:T(8,128)(2,1)S(1)} %copy-done, s32[]{:T(128)S(6)} %select_n.142, ...), kind=kOutput, calls=%fused_computation.51 | convolution fusion | flops 270565120 | bytes 8397828 | tf_op jit(solution)/shard_map/dot_general | solution.py:40
  247.7 16.2 %reduce-scatter.13.cloned.1.call-done = bf16[64,256]{1,0:T(8,128)(2,1)} async-done(((bf16[256,256]{1,0:T(8,128)(2,1)}), bf16[64,256]{1,0:T(8,128)(2,1)}) %reduce-scatter.13.cloned.1.call-update) | async-done | bytes 32784 | tf_op jit(solution)/shard_map/reduce_scatter | solution.py:232
  267.9 13.6 %all_gather.14 = bf16[256,256]{1,0:T(8,128)(2,1)S(1)} all-gather(bf16[64,256]{1,0:T(8,128)(2,1)S(1)} %collective-permute-done.2), channel_id=1, replica_groups=mesh['groups'=2,'segment'=4,'head'=4] {'head'}, dimensions={0}, use_global_device_ids=true | all-gather | bytes 163840 | tf_op jit(solution)/shard_map/all_gather | solution.py:241
  284.4 5.0 %fusion.15 = (f32[8,256]{1,0:T(8,128)}, f32[256,256,8]{1,0,2:T(8,128)}) fusion(f32[8,256]{1,0:T(8,128)} %get-tuple-element.6, f32[256,256,8]{1,0,2:T(8,128)} %copy-done.10, pred[256,256]{0,1:T(8,128)(4,1)S(1)} %copy-done.31, bf16[256,2048]{1,0:T(8,128)(2,1)} %copy-done.13, bf16[1,2048,512]{2,1,0:T(8,128)(2,1)S(1)} %copy-done, s32[]{:T(128)S(6)} %select_n.142, ...), kind=kOutput, calls=%fused_computation.32 | convolution fusion | flops 271087616 | bytes 6373380 | tf_op jit(solution)/shard_map/iknd,jkd->knij/dot_general | solution.py:110
  289.4 4.0 convert_bitcast_fusion.1
  310.1 5.1 %multiply_reduce_fusion.2 = (f32[256]{0:T(256)S(1)}, f32[256,2048]{1,0:T(8,128)}) fusion(f32[256,2048]{1,0:T(8,128)} %copy-done.3, f32[2048]{0:T(1024)S(1)} %bitcast.679, f32[256,2048]{1,0:T(8,128)} %convolution_add_fusion.3, bf16[1,2048,512]{2,1,0:T(8,128)(2,1)S(1)} %copy-done, s32[]{:T(128)S(6)} %select_n.142, bf16[256,8,128]{2,1,0:T(8,128)(2,1)} %bitcast.671, ...), kind=kOutput, calls=%fused_computation.47 | convolution fusion | flops 270565120 | bytes 8397828 | tf_op jit(solution)/shard_map/dot_general | solution.py:40
  323.9 12.9 %reduce-scatter.15.cloned.1.call-done = bf16[64,256]{1,0:T(8,128)(2,1)} async-done(((bf16[256,256]{1,0:T(8,128)(2,1)}), bf16[64,256]{1,0:T(8,128)(2,1)}) %reduce-scatter.15.cloned.1.call-update) | async-done | bytes 32784 | tf_op jit(solution)/shard_map/reduce_scatter | solution.py:232
  341.0 13.5 %all_gather.15 = bf16[256,256]{1,0:T(8,128)(2,1)S(1)} all-gather(bf16[64,256]{1,0:T(8,128)(2,1)S(1)} %collective-permute-done.3), channel_id=1, replica_groups=mesh['groups'=2,'segment'=4,'head'=4] {'head'}, dimensions={0}, use_global_device_ids=true | all-gather | bytes 163840 | tf_op jit(solution)/shard_map/all_gather | solution.py:241
  357.5 5.4 %fusion.11 = (f32[8,256]{1,0:T(8,128)S(1)}, f32[8,256]{1,0:T(8,128)S(1)}, f32[256,256,8]{1,0,2:T(8,128)}) fusion(f32[8,256]{1,0:T(8,128)S(1)} %copy-done.70, f32[256,256,8]{1,0,2:T(8,128)} %get-tuple-element.76, pred[256,256]{0,1:T(8,128)(4,1)S(1)} %copy-done.32, f32[256,256,8]{1,0,2:T(8,128)} %fusion.101, bf16[256,2048]{1,0:T(8,128)(2,1)} %copy-done.22, ...), kind=kOutput, calls=%fused_computation.26 | convolution fusion | flops 272658432 | bytes 8478724 | tf_op jit(solution)/shard_map/iknd,jkd->knij/dot_general | solution.py:110
  362.9 4.0 convert_bitcast_fusion
  370.3 3.8 convolution_convert_fusion.3
  387.3 5.1 %multiply_reduce_fusion = (f32[256]{0:T(256)S(1)}, f32[256,2048]{1,0:T(8,128)}) fusion(f32[256,2048]{1,0:T(8,128)} %copy-done.2, f32[2048]{0:T(1024)S(1)} %bitcast.680, f32[256,2048]{1,0:T(8,128)} %convolution_add_fusion.1, bf16[1,2048,512]{2,1,0:T(8,128)(2,1)S(1)} %copy-done, s32[]{:T(128)S(6)} %select_n.142, bf16[256,8,128]{2,1,0:T(8,128)(2,1)} %bitcast.670, ...), kind=kOutput, calls=%fused_computation.43 | convolution fusion | flops 270565120 | bytes 8397828 | tf_op jit(solution)/shard_map/dot_general | solution.py:40
  399.7 17.7 %reduce-scatter.17.cloned.1.call-done = bf16[64,256]{1,0:T(8,128)(2,1)} async-done(((bf16[256,256]{1,0:T(8,128)(2,1)}), bf16[64,256]{1,0:T(8,128)(2,1)}) %reduce-scatter.17.cloned.1.call-update) | async-done | bytes 32784 | tf_op jit(solution)/shard_map/reduce_scatter | solution.py:232
  (295 shorter events, 170.6 us)
Async XLA Ops:
  7.2 81.5 %copy-start = (bf16[1,2048,512]{2,1,0:T(8,128)(2,1)S(1)}, bf16[1,2048,512]{2,1,0:T(8,128)(2,1)}, u32[]{:S(2)}) copy-start(bf16[1,2048,512]{2,1,0:T(8,128)(2,1)} %param.24) | copy-start | bytes 6291460
  7.2 53.6 %all-reduce.3.cloned.1.call-start = ((), (), s32[]{:S(2)}) async-start(), calls=%async_computation.6 | async-start | bytes 1572864 | tf_op jit(solution)/shard_map/psum | solution.py:187
  14.0 99.0 %reduce-scatter.7.cloned.1.call-start = ((), (), s32[]{:S(2)}) async-start(), calls=%async_computation.7 | async-start | bytes 163840 | tf_op jit(solution)/shard_map/reduce_scatter | solution.py:211
  20.3 7.3 %copy-start.1 = (bf16[1,256,2048]{2,1,0:T(8,128)(2,1)S(1)}, bf16[1,256,2048]{2,1,0:T(8,128)(2,1)}, u32[]{:S(2)}) copy-start(bf16[1,256,2048]{2,1,0:T(8,128)(2,1)} %param.19) | copy-start | bytes 3145732
  94.6 81.8 %reduce-scatter.9.cloned.1.call-start = ((), (), s32[]{:S(2)}) async-start(), calls=%async_computation.8 | async-start | bytes 163840 | tf_op jit(solution)/shard_map/reduce_scatter | solution.py:211
  113.9 2.1 collective-permute-start
  115.8 17.6 %copy-start.68 = (f32[256]{0:T(256)}, f32[256]{0:T(256)S(1)}, u32[]{:S(2)}) copy-start(f32[256]{0:T(256)S(1)} %get-tuple-element.33) | copy-start | bytes 3076
  134.1 5.6 %copy-start.13 = (bf16[256,2048]{1,0:T(8,128)(2,1)}, bf16[256,2048]{1,0:T(8,128)(2,1)S(1)}, u32[]{:S(2)}) copy-start(bf16[256,2048]{1,0:T(8,128)(2,1)S(1)} %get-tuple-element.19) | copy-start | bytes 3145732
  134.1 6.2 %copy-start.15 = (bf16[256,2048]{1,0:T(8,128)(2,1)}, bf16[256,2048]{1,0:T(8,128)(2,1)S(1)}, u32[]{:S(2)}) copy-start(bf16[256,2048]{1,0:T(8,128)(2,1)S(1)} %get-tuple-element.20) | copy-start | bytes 3145732
  134.1 8.6 %copy-start.14 = (bf16[256,2048]{1,0:T(8,128)(2,1)}, bf16[256,2048]{1,0:T(8,128)(2,1)S(1)}, u32[]{:S(2)}) copy-start(bf16[256,2048]{1,0:T(8,128)(2,1)S(1)} %get-tuple-element.21) | copy-start | bytes 3145732
  155.3 108.6 %reduce-scatter.13.cloned.1.call-start = ((), (), s32[]{:S(2)}) async-start(), calls=%async_computation.10 | async-start | bytes 163840 | tf_op jit(solution)/shard_map/reduce_scatter | solution.py:232
  177.2 3.1 collective-permute-start.1
  180.3 23.6 %copy-start.10 = (f32[256,256,8]{1,0,2:T(8,128)}, f32[256,256,8]{1,0,2:T(8,128)S(1)}, u32[]{:S(2)}) copy-start(f32[256,256,8]{1,0,2:T(8,128)S(1)} %fusion.142) | copy-start | bytes 6291460
  180.3 15.2 %copy-start.25 = (bf16[256,256]{1,0:T(8,128)(2,1)S(1)}, bf16[256,256]{1,0:T(8,128)(2,1)}, u32[]{:S(2)}) copy-start(bf16[256,256]{1,0:T(8,128)(2,1)} %copy-done.23) | copy-start | bytes 393220
  244.0 40.4 %copy-start.31 = (pred[256,256]{0,1:T(8,128)(4,1)S(1)}, pred[256,256]{0,1:T(8,128)(4,1)}, u32[]{:S(2)}) copy-start(pred[256,256]{0,1:T(8,128)(4,1)} %iota_compare_fusion) | copy-start | bytes 196612
  244.0 92.8 %reduce-scatter.15.cloned.1.call-start = ((), (), s32[]{:S(2)}) async-start(), calls=%async_computation.11 | async-start | bytes 163840 | tf_op jit(solution)/shard_map/reduce_scatter | solution.py:232
  264.8 24.6 %copy-start.53 = (bf16[64,256]{1,0:T(8,128)(2,1)}, bf16[64,256]{1,0:T(8,128)(2,1)S(1)}, u32[]{:S(2)}) copy-start(bf16[64,256]{1,0:T(8,128)(2,1)S(1)} %add_convert_fusion.2) | copy-start | bytes 98308
  264.8 3.1 collective-permute-start.2
  318.8 78.7 %reduce-scatter.11.cloned.1.call-start = ((), (), s32[]{:S(2)}) async-start(), calls=%async_computation.9 | async-start | bytes 163840 | tf_op jit(solution)/shard_map/reduce_scatter | solution.py:211
  321.9 35.6 %copy-start.32 = (pred[256,256]{0,1:T(8,128)(4,1)S(1)}, pred[256,256]{0,1:T(8,128)(4,1)}, u32[]{:S(2)}) copy-start(pred[256,256]{0,1:T(8,128)(4,1)} %iota_compare_fusion) | copy-start | bytes 196612
  321.9 35.6 %copy-start.70 = (f32[8,256]{1,0:T(8,128)S(1)}, f32[8,256]{1,0:T(8,128)}, u32[]{:S(2)}) copy-start(f32[8,256]{1,0:T(8,128)} %get-tuple-element.4) | copy-start | bytes 24580
  337.6 25.2 %copy-start.54 = (bf16[64,256]{1,0:T(8,128)(2,1)}, bf16[64,256]{1,0:T(8,128)(2,1)S(1)}, u32[]{:S(2)}) copy-start(bf16[64,256]{1,0:T(8,128)(2,1)S(1)} %add_convert_fusion.1) | copy-start | bytes 98308
  337.7 3.4 collective-permute-start.3
  379.0 38.4 %reduce-scatter.17.cloned.1.call-start = ((), (), s32[]{:S(2)}) async-start(), calls=%async_computation.12 | async-start | bytes 163840 | tf_op jit(solution)/shard_map/reduce_scatter | solution.py:232
  (66 other events, 205.4 us)
Sparse Core Ops, SparseCore 0:
  14.1 46.6 all-reduce.2
  94.7 18.3 reduce-scatter.6
  155.4 20.8 reduce-scatter.8
  244.1 19.7 reduce-scatter.12
  318.9 17.8 reduce-scatter.14
  379.1 18.3 reduce-scatter.10
  399.7 17.6 reduce-scatter.16
